TPU v7x, 256 devices: a whole 4x4x8 slice. The times are simulated.
256 devices in a mesh: dp: 16 (over x, y), seq: 8 (over z_hi, core), mp: 2 (over z_lo).
Axes of the slice: x: 4, y: 4, z: 8 (z_hi: 4, z_lo: 2; z = z_hi * 2 + z_lo), core: 2. Of those that a mesh axis runs over, the one named last changes fastest.
Arguments:
- hidden_states: bfloat16 [8192, 2048], P(('dp', 'seq')), may hold values from -6 to 6
- embeddings: bfloat16 [8192, 2048], P(('dp', 'seq')), may hold values from -6 to 6
- norm_gain: float32 [4096], replicated, may hold values from 0.1 to 1.9
- input_weights: bfloat16 [4096, 3, 2, 2048], P('dp', None, 'mp', 'seq'), may hold values from -0.09375 to 0.09375
- adapter_down: bfloat16 [4096, 384], P(('seq', 'mp')), may hold values from -0.09375 to 0.09375
- adapter_up: bfloat16 [3, 128, 2, 2048], P(None, None, 'mp', 'seq'), may hold values from -0.5 to 0.5
- output_weights: bfloat16 [2, 2048, 2048], P('mp', 'seq', 'dp'), may hold values from -3 to 3
- own_keys: bfloat16 [16, 8192, 4096], P('dp', 'seq', 'mp'), may hold values from -164 to 164
- own_values: bfloat16 [16, 8192, 4096], P('dp', 'seq', 'mp'), may hold values from -6 to 6
- shared_keys: bfloat16 [2, 1024, 4096], P(None, 'seq', 'mp'), may hold values from -164 to 164
- shared_values: bfloat16 [2, 1024, 4096], P(None, 'seq', 'mp'), may hold values from -6 to 6
- cached_lengths: int32 [16], P('dp'), may hold values from 1 to 8192, 65536 in all
- prompt_group: int32 [16], P('dp'), may hold values from 0 to 1
- slot_pages: int32 [16, 128], P('dp', 'seq'), may hold values from 0 to 127, as said below
- padding_mask: int32 [8192], P(('dp', 'seq', 'mp')), may hold values from 0 to 1, as said below
Outputs:
- mixed: bfloat16 [8192, 2048], P(('dp', 'seq', 'mp'))
Inputs may be any that keep to these rules, and one draw needn't show every extreme that they name: `slot_pages`: row r maps the 128 page slots of request r one to one onto its pages: slot u holds page (u + c * 16) mod 128 for a whole number c of request r; page p holds own positions p * 64 to p * 64 + 63. `padding_mask`: within each request's 512 tokens the ones come first, then the zeros; at least 128 ones.
All inputs are finite; a program needn't handle non-finite values. No bound on the sum of `cached_lengths` on one device may be relied on, other than what follows from the above.
Results may differ from a plain program's by a relative error of at most 0.025.
The roundings to bfloat16 on the way count: a program that leaves them out, or rounds other values in their place, can miss the bound.
Values may be sent and summed in bfloat16 or wider, within the bound.
A program may use at most 128 MiB of HBM per device.

v0:
```python
import math

import jax
import jax.numpy as jnp
from jax import lax
from jax.sharding import PartitionSpec as P

HD = 128
PAGE = 64


eps = 1e-05
neg_fill = -1e30
head_block = 4


def joined_2(array, axis, combine):
    everything = jax.tree.map(lambda part: lax.all_gather(part, axis), array)
    leading = jax.tree.map(lambda part: part[0], everything)

    def hop(k, so_far):
        return combine(so_far, jax.tree.map(lambda part: part[k], everything))

    return lax.fori_loop(1, lax.axis_size(axis), hop, leading)


def normalize(hidden_states, embeddings, norm_gain):
    joined = jnp.concatenate([hidden_states, embeddings], axis=1).astype(jnp.float32)
    factor = lax.rsqrt(jnp.mean(joined * joined, axis=1, keepdims=True) + eps)
    return (joined * factor * norm_gain).astype(jnp.bfloat16)


def block_partial(queries, keys, values, usable):
    head_count = queries.shape[1]
    group_size = min(head_block, head_count)
    scaling = 1.0 / math.sqrt(queries.shape[2])

    def one_group(group_index):
        offset = group_index * group_size
        query_part = lax.dynamic_slice_in_dim(queries, offset, group_size, 1)
        key_part = lax.dynamic_slice_in_dim(keys, offset, group_size, 1)
        value_part = lax.dynamic_slice_in_dim(values, offset, group_size, 1)
        scores = (
            jnp.einsum("ihd,jhd->hij", query_part, key_part, preferred_element_type=jnp.float32)
            * scaling
        )
        scores = jnp.where(usable[None], scores, neg_fill)
        peak_score = jnp.max(scores, axis=2)
        exponent = jnp.exp(scores - peak_score[:, :, None])
        totals = jnp.sum(exponent, axis=2)
        weighted = jnp.einsum(
            "hij,jhd->ihd",
            exponent.astype(jnp.bfloat16),
            value_part,
            preferred_element_type=jnp.float32,
        )
        weighted = weighted / jnp.transpose(totals)[:, :, None]
        return (weighted.astype(jnp.bfloat16), jnp.transpose(peak_score), jnp.transpose(totals))

    outputs, peak_rows, total_rows = lax.map(one_group, jnp.arange(head_count // group_size))
    row_count = queries.shape[0]
    outputs = jnp.transpose(outputs, (1, 0, 2, 3)).reshape(row_count, head_count, queries.shape[2])
    peak_rows = jnp.transpose(peak_rows, (1, 0, 2)).reshape(row_count, head_count)
    total_rows = jnp.transpose(total_rows, (1, 0, 2)).reshape(row_count, head_count)
    return (outputs, peak_rows, total_rows)


def join_partials(earlier, later):
    out_first, peak_first, total_first = earlier
    out_second, peak_second, total_second = later
    highest = jnp.maximum(peak_first, peak_second)
    weight_first = total_first * jnp.exp(peak_first - highest)
    weight_second = total_second * jnp.exp(peak_second - highest)
    summed = weight_first + weight_second
    joined = (weight_first[..., None] * out_first + weight_second[..., None] * out_second) / summed[
        ..., None
    ]
    return (joined, highest, summed)


def fold_partials(outputs, peak_scores, totals):
    highest = jnp.max(peak_scores, axis=0)
    weight = totals * jnp.exp(peak_scores - highest)
    return jnp.sum(weight[..., None] * outputs, axis=0) / jnp.sum(weight, axis=0)[..., None]


def shards(
    hidden_states,
    embeddings,
    norm_gain,
    input_weights,
    adapter_down,
    adapter_up,
    output_weights,
    own_keys,
    own_values,
    shared_keys,
    shared_values,
    cached_lengths,
    prompt_group,
    slot_pages,
    padding_mask,
):
    normed = normalize(hidden_states, embeddings, norm_gain)
    gathered = lax.all_gather(normed, "seq", axis=0, tiled=True)
    new_count = gathered.shape[0]
    columns = gathered
    low_sum = jnp.dot(
        columns,
        lax.all_gather(adapter_down, ("seq", "mp"), axis=0, tiled=True),
        preferred_element_type=jnp.float32,
    )
    low_rank = low_sum.astype(jnp.bfloat16)
    width = input_weights.shape[3]
    piece = lax.all_gather(input_weights, "dp", axis=0, tiled=True)
    columns = gathered
    base_terms = jnp.dot(
        columns, piece.reshape(piece.shape[0], 3 * width), preferred_element_type=jnp.float32
    )
    rank_size = adapter_up.shape[1]
    lifted = jnp.einsum(
        "ipr,prc->ipc",
        low_rank.reshape(new_count, 3, rank_size),
        adapter_up[:, :, 0, :],
        preferred_element_type=jnp.float32,
    )
    projected = (base_terms.reshape(new_count, 3, width) + lifted).astype(jnp.bfloat16)
    query_local = projected[:, 0]
    key_local = projected[:, 1]
    value_local = projected[:, 2]
    local_heads = width // HD
    query_all = lax.all_gather(query_local, "seq", axis=1, tiled=True)
    mp_heads = query_all.shape[1] // HD
    group_index = prompt_group[0]
    shared_k = lax.dynamic_index_in_dim(shared_keys, group_index, 0, keepdims=False)
    shared_v = lax.dynamic_index_in_dim(shared_values, group_index, 0, keepdims=False)
    slot_count = own_keys.shape[1]
    cache_keys = jnp.concatenate([own_keys[0], shared_k], axis=0).reshape(-1, mp_heads, HD)
    cache_values = jnp.concatenate([own_values[0], shared_v], axis=0).reshape(-1, mp_heads, HD)
    positions = (
        jnp.repeat(slot_pages[0], PAGE, total_repeat_length=slot_count) * PAGE
        + jnp.arange(slot_count, dtype=jnp.int32) % PAGE
    )
    usable = jnp.concatenate(
        [positions < cached_lengths[0], jnp.ones((shared_k.shape[0],), dtype=jnp.bool_)]
    )[None, :]
    cache_out, cache_peak, cache_total = block_partial(
        query_all.reshape(new_count, mp_heads, HD), cache_keys, cache_values, usable
    )
    places = jnp.arange(new_count, dtype=jnp.int32)
    causal = places[:, None] >= places[None, :]
    new_out, new_peak, new_total = block_partial(
        query_local.reshape(new_count, local_heads, HD),
        key_local.reshape(new_count, local_heads, HD),
        value_local.reshape(new_count, local_heads, HD),
        causal,
    )
    merged_out, merged_peak, merged_total = joined_2(
        (cache_out.astype(jnp.float32), cache_peak, cache_total), "seq", join_partials
    )
    first_head = lax.axis_index("seq") * local_heads
    own_out = lax.dynamic_slice_in_dim(merged_out, first_head, local_heads, 1)
    own_peak = lax.dynamic_slice_in_dim(merged_peak, first_head, local_heads, 1)
    own_total = lax.dynamic_slice_in_dim(merged_total, first_head, local_heads, 1)
    outputs = jnp.stack([own_out, new_out.astype(jnp.float32)])
    peak_scores = jnp.stack([own_peak, new_peak])
    totals = jnp.stack([own_total, new_total])
    attended = (
        fold_partials(outputs, peak_scores, totals)
        .astype(jnp.bfloat16)
        .reshape(new_count, local_heads * HD)
    )
    out_matrix = lax.all_gather(output_weights, "dp", axis=2, tiled=True)[0]
    summed = lax.psum_scatter(
        jnp.dot(attended, out_matrix, preferred_element_type=jnp.float32).astype(jnp.bfloat16),
        ("seq", "mp"),
        scatter_dimension=0,
        tiled=True,
    ).astype(jnp.float32)
    return (padding_mask.astype(jnp.float32)[:, None] * summed).astype(jnp.bfloat16)


def solution(mesh):
    placed = (
        P(("dp", "seq"), None),
        P(("dp", "seq"), None),
        P(),
        P("dp", None, "mp", "seq"),
        P(("seq", "mp"), None),
        P(None, None, "mp", "seq"),
        P("mp", "seq", "dp"),
        P("dp", "seq", "mp"),
        P("dp", "seq", "mp"),
        P(None, "seq", "mp"),
        P(None, "seq", "mp"),
        P("dp"),
        P("dp"),
        P("dp", "seq"),
        P(("dp", "seq", "mp")),
    )
    return jax.shard_map(
        shards, mesh=mesh, in_specs=placed, out_specs=P(("dp", "seq", "mp"), None), check_vma=False
    )
```

profile of v0, /device:TPU:1, one launch (start us, length us, event | category | flops | bytes accessed | tf_op | source)
XLA Modules:
  0.0 744.2 jit_solution(12947220724132167045)
XLA Ops:
  6.5 0.7 all-gather.12.cloned.1.call-update
  7.3 1.2 fusion.45
  8.6 2.0 fusion.47
  10.7 1.9 copy.54
  12.6 64.0 %all-gather.12.cloned.1.call-done = bf16[4096,384]{1,0:T(8,128)(2,1)} async-done(((bf16[256,384]{1,0:T(8,128)(2,1)}), bf16[4096,384]{1,0:T(8,128)(2,1)}) %all-gather.12.cloned.1.call-update) | async-done | bytes 3145744 | tf_op jit(solution)/shard_map/all_gather | solution.py:110
  76.6 54.6 %all-gather.8.cloned.1.call-done = bf16[512,4096]{1,0:T(8,128)(2,1)} async-done(((bf16[64,4096]{1,0:T(8,128)(2,1)}), bf16[512,4096]{1,0:T(8,128)(2,1)}) %all-gather.8.cloned.1.call-update) | async-done | bytes 4194320 | tf_op jit(solution)/shard_map/all_gather | solution.py:105
  131.2 5.0 convolution_convert_fusion.1
  136.2 65.8 %all-gather.10.cloned.1.call-done = bf16[4096,3,1,256]{0,3,1,2:T(8,128)(2,1)} async-done(((bf16[256,3,1,256]{0,3,1,2:T(8,128)(2,1)}), bf16[4096,3,1,256]{0,3,1,2:T(8,128)(2,1)}) %all-gather.10.cloned.1.call-update) | async-done | bytes 6291472 | tf_op jit(solution)/shard_map/all_gather | solution.py:115
  202.0 6.8 fusion.34
  208.9 0.4 fusion.40
  209.3 0.9 fusion.67
  210.2 0.2 all-gather.14.cloned.1.call-start
  211.1 2.2 constant_dynamic-slice_fusion.4
  213.3 0.3 copy.53
  213.5 6.5 copy.52
  220.7 1.3 copy.81
  222.0 6.4 copy.57
  228.5 0.7 fusion.68
  229.3 4.3 compare_select_fusion.1
  233.7 5.6 fusion.58
  239.4 5.1 pad_maximum_fusion
  244.5 2.8 pad_maximum_fusion.1
  247.3 0.4 all-gather.18.cloned.1.call-done
  247.7 42.9 %while.40 = (s32[]{:T(128)}, bf16[4,512,4,128]{1,3,2,0:T(8,128)(2,1)S(1)}, f32[4,512,4]{1,2,0:T(4,128)S(1)}, f32[4,512,4]{1,2,0:T(4,128)S(1)}, s32[4]{0:T(128)S(...) while((s32[]{:T(128)}, ...), condition=%wide.region_4.5_spmd, body=%wide.region_1.0_spmd.sunk | while | flops 1234432000 | bytes 31798732 | solution.py:60
  247.7 0.6 dynamic_slice.107
  248.9 3.2 fusion.85
  252.2 2.3 fusion.86
  254.5 3.9 fusion.87
  258.4 0.6 dynamic_slice.107
  259.7 3.2 fusion.85
  262.9 2.3 fusion.86
  265.2 3.9 fusion.87
  269.1 0.6 dynamic_slice.107
  270.4 3.2 fusion.85
  273.7 2.3 fusion.86
  275.9 3.9 fusion.87
  279.9 0.6 dynamic_slice.107
  281.1 3.2 fusion.85
  284.4 2.3 fusion.86
  286.7 3.9 fusion.87
  290.6 2.5 convert_bitcast_fusion
  293.1 5.5 copy.61
  298.6 0.5 all-gather.16.cloned.1.call-update
  299.6 0.6 fusion.37
  300.2 0.5 fusion.39
  300.7 0.7 fusion.44
  301.5 18.6 %all_gather.30 = f32[8,512,16]{1,2,0:T(8,128)S(1)} all-gather(f32[1,512,16]{1,2,0:T(8,128)S(1)} %all_gather_reshape.6), channel_id=1, replica_groups=mesh['dp'=16,'seq'=8,'mp'=2] {'seq'}, dimensions={0}, use_global_device_ids=true | all-gather | bytes 294912 | tf_op jit(solution)/shard_map/all_gather | solution.py:18
  320.3 17.8 %all_gather.31 = f32[8,512,16]{1,2,0:T(8,128)S(1)} all-gather(f32[1,512,16]{1,2,0:T(8,128)S(1)} %all_gather_reshape.7), channel_id=1, replica_groups=mesh['dp'=16,'seq'=8,'mp'=2] {'seq'}, dimensions={0}, use_global_device_ids=true | all-gather | bytes 294912 | tf_op jit(solution)/shard_map/all_gather | solution.py:18
  338.2 261.0 %all-gather.14.cloned.1.call-done = f32[8,512,16,128]{3,2,1,0:T(8,128)} async-done(((f32[1,512,16,128]{3,2,1,0:T(8,128)}), f32[8,512,16,128]{3,2,1,0:T(8,128)}) %all-gather.14.cloned.1.call-update) | async-done | bytes 33554448 | tf_op jit(solution)/shard_map/all_gather | solution.py:18
  599.2 4.5 slice_bitcast_fusion
  603.7 66.2 %while.41 = (s32[]{:T(128)}, f32[512,16,128]{2,1,0:T(8,128)}, f32[512,16]{1,0:T(8,128)S(1)}, f32[512,16]{1,0:T(8,128)S(1)}, f32[8,512,16]{1,2,0:T(8,128)S(1)}, /...) while((s32[]{:T(128)}, f32[512,16,128]{2,1,0:T(8,128)}, ...), condition=%wide.region_6.7_spmd, body=%wide.region_5.6_spmd.sunk | while | flops 4243461 | bytes 13205655 | solution.py:24
  604.0 0.2 fusion.88
  604.2 9.0 %fusion.89 = f32[512,16,128]{2,1,0:T(8,128)} fusion(f32[8,512,16,128]{3,2,1,0:T(8,128)} %get-tuple-element.580, s32[]{:T(128)S(6)} %select_n.128, f32[512,16,128]{2,1,0:T(8,128)} %get-tuple-element.565, f32[512,16]{1,0:T(8,128)S(1)} %get-tuple-element.577, f32[512,16]{1,0:T(8,128)S(1)} %get-tuple-element.512, f32[512,16]{1,0:T(8,128)S(1)} %get-tuple-element.513), kind=kLoop, calls=%fused_computation.23.clone.1 | loop fusion | flops 4194304 | bytes 12681220 | tf_op jit(solution)/shard_map/while/body/eval_jaxpr/div | solution.py:75
  613.4 0.2 fusion.88
  613.7 9.0 %fusion.89 = f32[512,16,128]{2,1,0:T(8,128)} fusion(f32[8,512,16,128]{3,2,1,0:T(8,128)} %get-tuple-element.580, s32[]{:T(128)S(6)} %select_n.128, f32[512,16,128]{2,1,0:T(8,128)} %get-tuple-element.565, f32[512,16]{1,0:T(8,128)S(1)} %get-tuple-element.577, f32[512,16]{1,0:T(8,128)S(1)} %get-tuple-element.512, f32[512,16]{1,0:T(8,128)S(1)} %get-tuple-element.513), kind=kLoop, calls=%fused_computation.23.clone.1 | loop fusion | flops 4194304 | bytes 12681220 | tf_op jit(solution)/shard_map/while/body/eval_jaxpr/div | solution.py:75
  623.1 8.9 %fusion.89 = f32[512,16,128]{2,1,0:T(8,128)} fusion(f32[8,512,16,128]{3,2,1,0:T(8,128)} %get-tuple-element.580, s32[]{:T(128)S(6)} %select_n.128, f32[512,16,128]{2,1,0:T(8,128)} %get-tuple-element.565, f32[512,16]{1,0:T(8,128)S(1)} %get-tuple-element.577, f32[512,16]{1,0:T(8,128)S(1)} %get-tuple-element.512, f32[512,16]{1,0:T(8,128)S(1)} %get-tuple-element.513), kind=kLoop, calls=%fused_computation.23.clone.1 | loop fusion | flops 4194304 | bytes 12681220 | tf_op jit(solution)/shard_map/while/body/eval_jaxpr/div | solution.py:75
  632.6 9.0 %fusion.89 = f32[512,16,128]{2,1,0:T(8,128)} fusion(f32[8,512,16,128]{3,2,1,0:T(8,128)} %get-tuple-element.580, s32[]{:T(128)S(6)} %select_n.128, f32[512,16,128]{2,1,0:T(8,128)} %get-tuple-element.565, f32[512,16]{1,0:T(8,128)S(1)} %get-tuple-element.577, f32[512,16]{1,0:T(8,128)S(1)} %get-tuple-element.512, f32[512,16]{1,0:T(8,128)S(1)} %get-tuple-element.513), kind=kLoop, calls=%fused_computation.23.clone.1 | loop fusion | flops 4194304 | bytes 12681220 | tf_op jit(solution)/shard_map/while/body/eval_jaxpr/div | solution.py:75
  642.0 9.0 %fusion.89 = f32[512,16,128]{2,1,0:T(8,128)} fusion(f32[8,512,16,128]{3,2,1,0:T(8,128)} %get-tuple-element.580, s32[]{:T(128)S(6)} %select_n.128, f32[512,16,128]{2,1,0:T(8,128)} %get-tuple-element.565, f32[512,16]{1,0:T(8,128)S(1)} %get-tuple-element.577, f32[512,16]{1,0:T(8,128)S(1)} %get-tuple-element.512, f32[512,16]{1,0:T(8,128)S(1)} %get-tuple-element.513), kind=kLoop, calls=%fused_computation.23.clone.1 | loop fusion | flops 4194304 | bytes 12681220 | tf_op jit(solution)/shard_map/while/body/eval_jaxpr/div | solution.py:75
  651.5 8.9 %fusion.89 = f32[512,16,128]{2,1,0:T(8,128)} fusion(f32[8,512,16,128]{3,2,1,0:T(8,128)} %get-tuple-element.580, s32[]{:T(128)S(6)} %select_n.128, f32[512,16,128]{2,1,0:T(8,128)} %get-tuple-element.565, f32[512,16]{1,0:T(8,128)S(1)} %get-tuple-element.577, f32[512,16]{1,0:T(8,128)S(1)} %get-tuple-element.512, f32[512,16]{1,0:T(8,128)S(1)} %get-tuple-element.513), kind=kLoop, calls=%fused_computation.23.clone.1 | loop fusion | flops 4194304 | bytes 12681220 | tf_op jit(solution)/shard_map/while/body/eval_jaxpr/div | solution.py:75
  660.9 8.9 %fusion.89 = f32[512,16,128]{2,1,0:T(8,128)} fusion(f32[8,512,16,128]{3,2,1,0:T(8,128)} %get-tuple-element.580, s32[]{:T(128)S(6)} %select_n.128, f32[512,16,128]{2,1,0:T(8,128)} %get-tuple-element.565, f32[512,16]{1,0:T(8,128)S(1)} %get-tuple-element.577, f32[512,16]{1,0:T(8,128)S(1)} %get-tuple-element.512, f32[512,16]{1,0:T(8,128)S(1)} %get-tuple-element.513), kind=kLoop, calls=%fused_computation.23.clone.1 | loop fusion | flops 4194304 | bytes 12681220 | tf_op jit(solution)/shard_map/while/body/eval_jaxpr/div | solution.py:75
  669.9 1.8 constant_dynamic-slice_fusion.2
  672.5 3.3 convolution_convert_fusion
  675.9 59.8 %reduce-scatter.2.cloned.1.call-done = bf16[32,2048]{1,0:T(8,128)(2,1)} async-done(((bf16[512,2048]{1,0:T(8,128)(2,1)}), bf16[32,2048]{1,0:T(8,128)(2,1)}) %reduce-scatter.2.cloned.1.call-update) | async-done | bytes 131088 | tf_op jit(solution)/shard_map/reduce_scatter | solution.py:174
  735.7 1.6 multiply_convert_fusion
  (85 shorter events, 4.9 us)
Async XLA Ops:
  6.5 202.3 %copy-start = (bf16[3,128,1,256]{3,1,2,0:T(8,128)(2,1)S(1)}, bf16[3,128,1,256]{3,1,2,0:T(8,128)(2,1)}, u32[]{:S(2)}) copy-start(bf16[3,128,1,256]{3,1,2,0:T(8,128)(2,1)} %param.26) | copy-start | bytes 589828
  6.5 70.1 %all-gather.12.cloned.1.call-start = ((), (), s32[]{:S(2)}) async-start(), calls=%async_computation.3 | async-start | bytes 3342336 | tf_op jit(solution)/shard_map/all_gather | solution.py:110
  7.3 124.0 %all-gather.8.cloned.1.call-start = ((), (), s32[]{:S(2)}) async-start(), calls=%async_computation.1 | async-start | bytes 4718592 | tf_op jit(solution)/shard_map/all_gather | solution.py:105
  10.6 191.4 %all-gather.10.cloned.1.call-start = ((), (), s32[]{:S(2)}) async-start(), calls=%async_computation.2 | async-start | bytes 6684672 | tf_op jit(solution)/shard_map/all_gather | solution.py:115
  12.6 235.1 %all-gather.18.cloned.1.call-start = ((), (), s32[]{:S(2)}) async-start(), calls=%async_computation.7 | async-start | bytes 2359296 | tf_op jit(solution)/shard_map/all_gather | solution.py:132
  210.2 389.0 %all-gather.14.cloned.1.call-start = ((), (), s32[]{:S(2)}) async-start(), calls=%async_computation.4 | async-start | bytes 37748736 | tf_op jit(solution)/shard_map/all_gather | solution.py:18
  222.0 6.5 copy-start.6
  222.0 7.2 copy-start.7
  239.4 5.1 copy-start.2
  298.6 0.9 copy-start.3
  298.6 1.0 copy-start.4
  298.6 2.2 copy-start.5
  298.6 373.9 %all-gather.16.cloned.1.call-start = ((), (), s32[]{:S(2)}) async-start(), calls=%async_computation.5 | async-start | bytes 1114112 | tf_op jit(solution)/shard_map/all_gather | solution.py:173
  299.2 436.5 %reduce-scatter.2.cloned.1.call-start = ((), (), s32[]{:S(2)}) async-start(), calls=%async_computation.6 | async-start | bytes 2228224 | tf_op jit(solution)/shard_map/reduce_scatter | solution.py:174
  672.3 3.6 copy-start.8
  672.3 65.1 %copy-start.1 = (bf16[3,128,1,256]{3,1,2,0:T(8,128)(2,1)S(1)}, bf16[3,128,1,256]{3,1,2,0:T(8,128)(2,1)}, u32[]{:S(2)}) copy-start(bf16[3,128,1,256]{3,1,2,0:T(8,128)(2,1)} %param.26) | copy-start | bytes 589828
Sparse Core Ops, SparseCore 0:
  9.1 67.4 all-gather.11
  78.5 52.7 all-gather.7
  133.7 68.3 all-gather.9
  210.3 37.3 all-gather.17
  298.7 300.4 all-gather.13
  601.5 44.6 all-gather.15
  676.0 59.6 reduce-scatter.1
where the time goes:
time: 747 us; the launch traced here: 744 us
  waiting for transfers between devices  507 us (68%)
  other arithmetic  99.7 us (13%)
  matrix products  45.5 us (6%)
  local copies, waits for them, and re-layouts  37.5 us (5%)
  blocking collectives  36.4 us (5%)
  between operations  15.1 us (2%)
    all_gather x1, waiting for transfers between devices, joined_2(): everything = jax.tree.map(lambda part: lax.all_gather(part, axis), array)  261 us
    all_gather x1, waiting for transfers between devices, shards(): piece = lax.all_gather(input_weights, 'dp', axis=0, tiled=True)  65.8 us
    all_gather x1, waiting for transfers between devices, shards(): lax.all_gather(adapter_down, ('seq', 'mp'), axis=0, tiled=True)  64 us
    div x7, other arithmetic, join_partials(): (weight_first[..., None] * out_first + weight_second[..., None] * out_sec...  62.7 us
    reduce_scatter x1, waiting for transfers between devices, shards(): lax.psum_scatter(jnp.dot(attended, out_matrix, preferred_element_type=jnp...  59.8 us
    all_gather x1, waiting for transfers between devices, shards(): gathered = lax.all_gather(normed, 'seq', axis=0, tiled=True)  54.6 us
    all_gather x2, blocking collectives, joined_2(): everything = jax.tree.map(lambda part: lax.all_gather(part, axis), array)  36.4 us
    unnamed x22, local copies, waits for them, and re-layouts  16.5 us
  transfers between devices with their start and end apart: 7, of which 6 were waited for; matrix products, arithmetic and copies ran while one was open for 16% of the time, Pallas kernels for 0%

commit v1 on v0

v1 whole, which is shorter than its diff:
```python
import functools
import math

import jax
import jax.numpy as jnp
from jax import lax
from jax.experimental import pallas as pl
from jax.experimental.pallas import tpu as pltpu
from jax.sharding import PartitionSpec as P

HD = 128
PAGE = 64
MESH = pl.DeviceIdType.MESH
F32 = jnp.float32
BF16 = jnp.bfloat16

eps = 1e-05
neg_fill = -1e30


def normalize(hidden_states, embeddings, norm_gain):
    joined = jnp.concatenate([hidden_states, embeddings], axis=1).astype(jnp.float32)
    factor = lax.rsqrt(jnp.mean(joined * joined, axis=1, keepdims=True) + eps)
    return (joined * factor * norm_gain).astype(jnp.bfloat16)


def remote(src, dst, send, recv, target):
    return pltpu.make_async_remote_copy(
        src_ref=src, dst_ref=dst, send_sem=send, recv_sem=recv,
        device_id=target, device_id_type=MESH,
    )


def attend_tile(queries, keys, values, bias, scale):
    scores = lax.dot_general(queries, keys, (((1,), (1,)), ((), ())), preferred_element_type=F32)
    scores = scores + bias
    peak = jnp.max(scores, axis=1, keepdims=True)
    weights = jnp.exp2((scores - peak) * scale).astype(BF16)
    wide = jnp.concatenate([values, jnp.ones_like(values)], axis=1)
    both = jnp.dot(weights, wide, preferred_element_type=F32)
    total = both[:, HD:]
    return (both[:, :HD] / total).astype(BF16), peak * scale + jnp.log2(total)


def attention_kernel(
    length_ref, group_ref, pages_ref, q_ref, nk_ref, nv_ref, ok_ref, ov_ref, sk_ref, sv_ref,
    out_ref,
    kbuf, vbuf, skst, svst, bias, qbuf, osend, lsend, orecv, lrecv, orelay, lnew, onew,
    kv_loc, kv_snd, kv_rcv, sh_loc, sh_snd, sh_rcv, q_snd, q_rcv, o_snd, o_rcv, l_snd, l_rcv,
):
    seq_i, core = lax.axis_index("seq"), lax.rem(lax.axis_index("seq"), 2)
    zh = seq_i // 2
    places = kbuf.shape[0]
    own_count, shared_count = ok_ref.shape[1], sk_ref.shape[1]
    tokens, wide = q_ref.shape
    n_seq = 2 * places
    half = tokens // 2
    tile = min(128, half)
    scale = math.log2(math.e) / math.sqrt(HD)
    partner = {"seq": seq_i + 1 - 2 * core}
    above_i, below_i, far_i = (lax.rem(zh + k, places) for k in (1, places - 1, 2))
    above, below, far = ({"seq": 2 * i + core} for i in (above_i, below_i, far_i))

    barrier = pltpu.get_barrier_semaphore()
    for target in (partner, above, below, far):
        pl.semaphore_signal(barrier, inc=1, device_id=target, device_id_type=MESH)
    pl.semaphore_wait(barrier, 4)

    q_up = remote(q_ref, qbuf.at[zh], q_snd.at[0], q_rcv.at[0], above)
    q_down = remote(q_ref, qbuf.at[zh], q_snd.at[1], q_rcv.at[1], below)
    q_up.start()
    q_down.start()

    local, out_going = [], []
    for kv, (source, buffer) in enumerate(((ok_ref, kbuf), (ov_ref, vbuf))):
        for j in range(places):
            mine = pl.ds(pl.multiple_of((2 * j + core) * wide, wide), wide)
            other = pl.ds(pl.multiple_of((2 * j + 1 - core) * wide, wide), wide)
            local.append(pltpu.make_async_copy(
                source.at[0, :, mine], buffer.at[j, pl.ds(0, own_count), :], kv_loc.at[kv, j]))
            out_going.append(remote(
                source.at[0, :, other], buffer.at[j, pl.ds(own_count, own_count), :],
                kv_snd.at[kv, j], kv_rcv.at[kv, j], partner))
    for kv, (source, buffer) in enumerate(((sk_ref, skst), (sv_ref, svst))):
        for j in range(places):
            mine = pl.ds(pl.multiple_of((2 * j + core) * wide, wide), wide)
            other = pl.ds(pl.multiple_of((2 * j + 1 - core) * wide, wide), wide)
            local.append(pltpu.make_async_copy(
                source.at[:, :, mine], buffer.at[0, j], sh_loc.at[kv, j]))
            out_going.append(remote(
                source.at[:, :, other], buffer.at[1, j],
                sh_snd.at[kv, j], sh_rcv.at[kv, j], partner))
    for copy in local + out_going:
        copy.start()

    keys_in_all = bias.shape[1]
    pages_here = pages_ref.shape[1]
    page_count = pages_here * n_seq
    first = pages_ref[0, 0]
    first_other = lax.rem(first + page_count + pages_here * (1 - 2 * core), page_count)
    spots = lax.broadcasted_iota(jnp.int32, bias.shape, 1)
    limit_own = length_ref[0] - first * PAGE
    limit_other = length_ref[0] - first_other * PAGE + own_count
    usable = (spots >= 2 * own_count) | (spots < jnp.where(spots < own_count, limit_own, limit_other))
    bias[...] = jnp.where(usable, 0.0, neg_fill)

    qbuf[zh] = q_ref[...]

    def new_tile(t, carry):
        rows = pl.ds(pl.multiple_of(t * tile, tile), tile)
        row_ids = t * tile + lax.broadcasted_iota(jnp.int32, (tile, tokens), 0)
        col_ids = lax.broadcasted_iota(jnp.int32, (tile, tokens), 1)
        masked = jnp.where(col_ids <= row_ids, 0.0, neg_fill)
        for l in range(wide // HD):
            lanes = slice(l * HD, (l + 1) * HD)
            o, lse = attend_tile(q_ref[rows, lanes], nk_ref[:, lanes], nv_ref[:, lanes], masked, scale)
            onew[rows, lanes] = o
            lnew[l, rows, :] = lse
        return carry

    lax.fori_loop(0, tokens // tile, new_tile, 0)

    q_up.wait_recv()
    relay_up = remote(
        qbuf.at[below_i, pl.ds(0, half), :], qbuf.at[below_i, pl.ds(0, half), :],
        q_snd.at[2], q_rcv.at[2], above)
    relay_up.start()
    q_down.wait_recv()
    relay_down = remote(
        qbuf.at[above_i, pl.ds(half, half), :], qbuf.at[above_i, pl.ds(half, half), :],
        q_snd.at[3], q_rcv.at[3], below)
    relay_down.start()

    for copy in local:
        copy.wait()
    for copy in out_going:
        copy.wait()
    group = group_ref[0]
    for w in range(2):
        spot = pl.ds(2 * own_count + w * shared_count, shared_count)
        for j in range(places):
            kbuf[j, spot, :] = skst[w, j, group]
            vbuf[j, spot, :] = svst[w, j, group]

    def block(j, start, count, o_ref, l_ref):
        def one(t, carry):
            rows = pl.ds(pl.multiple_of(start + t * tile, tile), tile)
            lses = []
            for l in range(wide // HD):
                lanes = slice(l * HD, (l + 1) * HD)
                o, lse = attend_tile(
                    qbuf[j, rows, lanes], kbuf[j, :, lanes], vbuf[j, :, lanes], bias[0:1, :], scale)
                o_ref[j, rows, lanes] = o
                lses.append(lse)
            lane = lax.broadcasted_iota(jnp.int32, (tile, HD), 1)
            turned = jnp.where(lane < HD // 2, lses[0], lses[1]).T
            l_ref[j, 0:1, rows] = turned[0:1]
            l_ref[j, 1:2, rows] = turned[HD // 2:HD // 2 + 1]
            return carry

        lax.fori_loop(0, count // tile, one, 0)

    lsend[...] = jnp.zeros_like(lsend)
    block(zh, 0, tokens, orecv, lrecv)
    sends = []

    def give(j, target, k):
        o = remote(osend.at[j], orecv.at[zh], o_snd.at[k], o_rcv.at[k], target)
        l = remote(lsend.at[j], lrecv.at[zh], l_snd.at[k], l_rcv.at[k], target)
        o.start()
        l.start()
        sends.extend((o, l))

    block(below_i, 0, tokens, osend, lsend)
    give(below_i, below, 0)
    block(above_i, 0, tokens, osend, lsend)
    give(above_i, above, 1)

    relay_up.wait_recv()
    block(far_i, 0, half, osend, lsend)
    out_up = remote(osend.at[far_i, pl.ds(0, half), :], orelay.at[0], o_snd.at[2], o_rcv.at[2], above)
    out_up.start()
    relay_down.wait_recv()
    block(far_i, half, half, osend, lsend)
    out_down = remote(osend.at[far_i, pl.ds(half, half), :], orelay.at[1], o_snd.at[3], o_rcv.at[3], below)
    out_down.start()
    l_far = remote(lsend.at[far_i], lrecv.at[zh], l_snd.at[2], l_rcv.at[2], far)
    l_far.start()

    out_up.wait_recv()
    pass_up = remote(orelay.at[0], orecv.at[below_i, pl.ds(0, half), :], o_snd.at[4], o_rcv.at[4], above)
    pass_up.start()
    out_down.wait_recv()
    pass_down = remote(orelay.at[1], orecv.at[above_i, pl.ds(half, half), :], o_snd.at[5], o_rcv.at[5], below)
    pass_down.start()

    for copy in sends:
        copy.wait_recv()
    l_far.wait_recv()
    pass_up.wait_recv()
    pass_down.wait_recv()

    def merge(t, carry):
        rows = pl.ds(pl.multiple_of(t * tile, tile), tile)
        stats = [lrecv[b, :, rows] for b in range(places)]
        stats.append(jnp.zeros((HD - 8 * places, tile), F32))
        columns = jnp.concatenate(stats, axis=0).T
        for l in range(wide // HD):
            lanes = slice(l * HD, (l + 1) * HD)
            lses = [jnp.broadcast_to(columns[:, 8 * b + l:8 * b + l + 1], (tile, HD)) for b in range(places)]
            lses.append(lnew[l, rows, :])
            highest = functools.reduce(jnp.maximum, lses)
            parts = [orecv[b, rows, lanes] for b in range(places)] + [onew[rows, lanes]]
            weights = [jnp.exp2(x - highest) for x in lses]
            summed = functools.reduce(jnp.add, [w * p.astype(F32) for w, p in zip(weights, parts)])
            out_ref[rows, lanes] = (summed / functools.reduce(jnp.add, weights)).astype(BF16)
        return carry

    lax.fori_loop(0, tokens // tile, merge, 0)

    for copy in (q_up, q_down, relay_up, relay_down, out_up, out_down, l_far, pass_up, pass_down):
        copy.wait_send()
    for copy in sends:
        copy.wait_send()


def attention(cached_lengths, prompt_group, slot_pages, q, nk, nv, own_keys, own_values, shared_keys, shared_values):
    tokens, wide = q.shape
    places = own_keys.shape[2] // wide // 2
    own_count, shared_count = own_keys.shape[1], shared_keys.shape[1]
    groups = shared_keys.shape[0]
    keys_in_all = 2 * (own_count + shared_count)
    half = tokens // 2
    heads = wide // HD
    smem = pl.BlockSpec(memory_space=pltpu.SMEM)
    vmem = pl.BlockSpec(memory_space=pltpu.VMEM)
    hbm = pl.BlockSpec(memory_space=pl.ANY)
    dma = pltpu.SemaphoreType.DMA
    return pl.pallas_call(
        attention_kernel,
        out_shape=jax.ShapeDtypeStruct((tokens, wide), BF16),
        in_specs=[smem] * 3 + [vmem] * 3 + [hbm] * 4,
        out_specs=vmem,
        scratch_shapes=[
            pltpu.VMEM((places, keys_in_all, wide), BF16),
            pltpu.VMEM((places, keys_in_all, wide), BF16),
            pltpu.VMEM((2, places, groups, shared_count, wide), BF16),
            pltpu.VMEM((2, places, groups, shared_count, wide), BF16),
            pltpu.VMEM((8, keys_in_all), F32),
            pltpu.VMEM((places, tokens, wide), BF16),
            pltpu.VMEM((places, tokens, wide), BF16),
            pltpu.VMEM((places, 8, tokens), F32),
            pltpu.VMEM((places, tokens, wide), BF16),
            pltpu.VMEM((places, 8, tokens), F32),
            pltpu.VMEM((2, half, wide), BF16),
            pltpu.VMEM((heads, tokens, HD), F32),
            pltpu.VMEM((tokens, wide), BF16),
            dma((2, places)), dma((2, places)), dma((2, places)),
            dma((2, places)), dma((2, places)), dma((2, places)),
            dma((4,)), dma((4,)), dma((6,)), dma((6,)), dma((3,)), dma((3,)),
        ],
        compiler_params=pltpu.CompilerParams(
            collective_id=0, has_side_effects=True, vmem_limit_bytes=60 * 2**20),
    )(cached_lengths, prompt_group, slot_pages, q, nk, nv, own_keys, own_values, shared_keys, shared_values)


def shards(
    hidden_states,
    embeddings,
    norm_gain,
    input_weights,
    adapter_down,
    adapter_up,
    output_weights,
    own_keys,
    own_values,
    shared_keys,
    shared_values,
    cached_lengths,
    prompt_group,
    slot_pages,
    padding_mask,
):
    normed = normalize(hidden_states, embeddings, norm_gain)
    gathered = lax.all_gather(normed, "seq", axis=0, tiled=True)
    new_count = gathered.shape[0]
    low_sum = jnp.dot(
        gathered,
        lax.all_gather(adapter_down, ("seq", "mp"), axis=0, tiled=True),
        preferred_element_type=jnp.float32,
    )
    low_rank = low_sum.astype(jnp.bfloat16)
    width = input_weights.shape[3]
    piece = lax.all_gather(input_weights, "dp", axis=0, tiled=True)
    base_terms = jnp.dot(
        gathered, piece.reshape(piece.shape[0], 3 * width), preferred_element_type=jnp.float32
    )
    rank_size = adapter_up.shape[1]
    lifted = jnp.einsum(
        "ipr,prc->ipc",
        low_rank.reshape(new_count, 3, rank_size),
        adapter_up[:, :, 0, :],
        preferred_element_type=jnp.float32,
    )
    projected = (base_terms.reshape(new_count, 3, width) + lifted).astype(jnp.bfloat16)
    attended = attention(
        cached_lengths, prompt_group, slot_pages,
        projected[:, 0], projected[:, 1], projected[:, 2],
        own_keys, own_values, shared_keys, shared_values)
    out_matrix = lax.all_gather(output_weights, "dp", axis=2, tiled=True)[0]
    summed = lax.psum_scatter(
        jnp.dot(attended, out_matrix, preferred_element_type=jnp.float32).astype(jnp.bfloat16),
        ("seq", "mp"),
        scatter_dimension=0,
        tiled=True,
    ).astype(jnp.float32)
    return (padding_mask.astype(jnp.float32)[:, None] * summed).astype(jnp.bfloat16)


def solution(mesh):
    placed = (
        P(("dp", "seq"), None),
        P(("dp", "seq"), None),
        P(),
        P("dp", None, "mp", "seq"),
        P(("seq", "mp"), None),
        P(None, None, "mp", "seq"),
        P("mp", "seq", "dp"),
        P("dp", "seq", "mp"),
        P("dp", "seq", "mp"),
        P(None, "seq", "mp"),
        P(None, "seq", "mp"),
        P("dp"),
        P("dp"),
        P("dp", "seq"),
        P(("dp", "seq", "mp")),
    )
    return jax.shard_map(
        shards, mesh=mesh, in_specs=placed, out_specs=P(("dp", "seq", "mp"), None), check_vma=False
    )
```

time: 747 us -> 346 us (0.46)
  waiting for transfers between devices: 507 us -> 244 us
  other arithmetic: 99.7 us -> 4.92 us
  Pallas kernels: 0 us -> 63.3 us
  blocking collectives: 36.4 us -> 0 us
  local copies, waits for them, and re-layouts: 37.5 us -> 2.83 us
  matrix products: 45.5 us -> 15.9 us
    all_gather x2 -> x0, waiting for transfers between devices: 261 us -> none  [the longest x1 261 us: joined_2(): everything = jax.tree.map(lambda part: lax.all_gather(part, axis), array)]
    pallas_call x0 -> x1, Pallas kernels: none -> 63.3 us  [attention(): pl.pallas_call(attention_kernel, out_shape=jax.ShapeDtypeStruct((tokens,...]
    div x7 -> x0, other arithmetic: 62.7 us -> none  [join_partials(): (weight_first[..., None] * out_first + weight_second[..., None] * out_sec...]
    all_gather x2 -> x0, blocking collectives: 36.4 us -> none  [joined_2(): everything = jax.tree.map(lambda part: lax.all_gather(part, axis), array)]
    dot_general x12 -> x2, matrix products: 41.8 us -> 12.1 us  [the longest x1 7.1 us: shards(): jnp.dot(gathered, piece.reshape(piece.shape[0], 3 * width), preferred_ele...]
    unnamed x22 -> x5, local copies, waits for them, and re-layouts: 16.5 us -> 1.93 us
    reduce_sum x7 -> x0, other arithmetic: 9.77 us -> none  [the longest x5 9.61 us: one_group(): totals = jnp.sum(exponent, axis=2)]
    dynamic_slice x31 -> x0, local copies, waits for them, and re-layouts: 8.99 us -> none  [the longest x4 2.55 us: block_partial(): lax.map(one_group, jnp.arange(head_count // group_size))]
  transfers between devices with their start and end apart: 7 -> 5, of which waited for: 6 -> 4; matrix products, arithmetic and copies ran while one was open for 16% -> 5% of each run, Pallas kernels for 0% -> 18%
where the time goes in v1:
time: 346 us; the launch traced here: 345 us
  waiting for transfers between devices  244 us (71%)
  Pallas kernels  63.3 us (18%)
  matrix products  15.9 us (5%)
  between operations  14.5 us (4%)
  other arithmetic  4.92 us (1%)
    all_gather x1, waiting for transfers between devices, shards(): piece = lax.all_gather(input_weights, 'dp', axis=0, tiled=True)  65.8 us
    pallas_call x1, Pallas kernels, attention(): pl.pallas_call(attention_kernel, out_shape=jax.ShapeDtypeStruct((tokens,...  63.3 us
    all_gather x1, waiting for transfers between devices, shards(): lax.all_gather(adapter_down, ('seq', 'mp'), axis=0, tiled=True)  62.1 us
    reduce_scatter x1, waiting for transfers between devices, shards(): lax.psum_scatter(jnp.dot(attended, out_matrix, preferred_element_type=jnp...  60 us
    all_gather x1, waiting for transfers between devices, shards(): gathered = lax.all_gather(normed, 'seq', axis=0, tiled=True)  54.6 us
    dot_general x1, matrix products, shards(): jnp.dot(gathered, piece.reshape(piece.shape[0], 3 * width), preferred_ele...  7.1 us
  transfers between devices with their start and end apart: 5, of which 4 were waited for; matrix products, arithmetic and copies ran while one was open for 5% of the time, Pallas kernels for 18%

profile of v1, /device:TPU:1, one launch (start us, length us, event | category | flops | bytes accessed | tf_op | source)
XLA Modules:
  0.0 345.4 jit_solution(8746413339800950471)
XLA Ops:
  6.5 0.0 copy-start
  6.5 0.0 all-gather.9.cloned.1.call-start
  6.5 0.7 all-gather.9.cloned.1.call-update
  7.3 0.0 all-gather.5.cloned.1.call-start
  7.3 1.2 fusion.4
  8.6 2.0 fusion.6
  10.6 0.0 all-gather.5.cloned.1.call-update
  10.6 0.0 all-gather.7.cloned.1.call-start
  10.7 1.9 copy.17
  12.6 0.0 all-gather.7.cloned.1.call-update
  12.6 0.0 all-gather.11.cloned.1.call-start
  12.7 0.5 all-gather.11.cloned.1.call-update
  13.2 0.0 reduce-scatter.2.cloned.1.call-start
  14.5 62.1 %all-gather.9.cloned.1.call-done = bf16[4096,384]{1,0:T(8,128)(2,1)} async-done(((bf16[256,384]{1,0:T(8,128)(2,1)}), bf16[4096,384]{1,0:T(8,128)(2,1)}) %all-gather.9.cloned.1.call-update) | async-done | bytes 3145744 | tf_op jit(solution)/shard_map/all_gather | solution.py:289
  76.6 54.6 %all-gather.5.cloned.1.call-done = bf16[512,4096]{1,0:T(8,128)(2,1)} async-done(((bf16[64,4096]{1,0:T(8,128)(2,1)}), bf16[512,4096]{1,0:T(8,128)(2,1)}) %all-gather.5.cloned.1.call-update) | async-done | bytes 4194320 | tf_op jit(solution)/shard_map/all_gather | solution.py:285
  131.2 5.0 %convolution_convert_fusion.1 = bf16[512,384]{0,1:T(8,128)(2,1)S(1)} fusion(bf16[512,4096]{1,0:T(8,128)(2,1)} %all-gather.5.cloned.1.call-done, bf16[4096,384]{1,0:T(8,128)(2,1)} %all-gather.9.cloned.1.call-done), kind=kOutput, calls=%fused_computation.8 | convolution fusion | flops 1610809344 | bytes 7733248 | tf_op jit(solution)/shard_map/dot_general | solution.py:287
  136.2 65.8 %all-gather.7.cloned.1.call-done = bf16[4096,3,1,256]{0,3,1,2:T(8,128)(2,1)} async-done(((bf16[256,3,1,256]{0,3,1,2:T(8,128)(2,1)}), bf16[4096,3,1,256]{0,3,1,2:T(8,128)(2,1)}) %all-gather.7.cloned.1.call-update) | async-done | bytes 6291472 | tf_op jit(solution)/shard_map/all_gather | solution.py:294
  202.0 7.1 %fusion = f32[512,3,256]{2,0,1:T(8,128)S(1)} fusion(bf16[4096,3,1,256]{0,3,1,2:T(8,128)(2,1)} %all-gather.7.cloned.1.call-done, bf16[512,4096]{1,0:T(8,128)(2,1)} %all-gather.5.cloned.1.call-done), kind=kOutput, calls=%fused_computation | convolution fusion | flops 3221225472 | bytes 12058624 | tf_op jit(solution)/shard_map/dot_general | solution.py:295
  209.1 0.0 copy-done
  209.1 0.4 fusion.3
  209.6 0.9 slice_bitcast_fusion
  210.5 63.3 %shard_map.145 = bf16[512,256]{1,0:T(8,128)(2,1)} custom-call(s32[1]{0:T(128)S(6)} %copy.20.length_ref, s32[1]{0:T(128)S(6)} %copy.21.group_ref, s32[1,16]{1,0:T(1,128)} %pages_ref.1, bf16[512,256]{1,0:T(8,128)(2,1)} %get-tuple-element.7.q_ref, bf16[512,256]{1,0:T(8,128)(2,1)} %get-tuple-element.6.nk_ref, bf16[512,256]{1,0:T(8,128)(2,1)} %get-tuple-element.5.nv_ref, ...), custom_call_target="tpu_custom_call" | custom-call | tf_op jit(solution)/shard_map/pallas_call | solution.py:239
  273.7 0.0 copy-start.1
  273.7 0.0 all-gather.11.cloned.1.call-done
  273.8 3.4 convolution_convert_fusion
  277.1 0.0 reduce-scatter.2.cloned.1.call-update
  277.2 0.0 copy-done.1
  277.2 60.0 %reduce-scatter.2.cloned.1.call-done = bf16[32,2048]{1,0:T(8,128)(2,1)} async-done(((bf16[512,2048]{1,0:T(8,128)(2,1)}), bf16[32,2048]{1,0:T(8,128)(2,1)}) %reduce-scatter.2.cloned.1.call-update) | async-done | bytes 131088 | tf_op jit(solution)/shard_map/reduce_scatter | solution.py:311
  337.2 1.6 multiply_convert_fusion
  (2 shorter events, 0.0 us)
Async XLA Ops:
  6.5 202.6 %copy-start = (bf16[3,128,1,256]{3,1,2,0:T(8,128)(2,1)S(1)}, bf16[3,128,1,256]{3,1,2,0:T(8,128)(2,1)}, u32[]{:S(2)}) copy-start(bf16[3,128,1,256]{3,1,2,0:T(8,128)(2,1)} %param.20) | copy-start | bytes 589828
  6.5 70.1 %all-gather.9.cloned.1.call-start = ((), (), s32[]{:S(2)}) async-start(), calls=%async_computation.3 | async-start | bytes 3342336 | tf_op jit(solution)/shard_map/all_gather | solution.py:289
  7.3 124.0 %all-gather.5.cloned.1.call-start = ((), (), s32[]{:S(2)}) async-start(), calls=%async_computation.1 | async-start | bytes 4718592 | tf_op jit(solution)/shard_map/all_gather | solution.py:285
  10.6 191.4 %all-gather.7.cloned.1.call-start = ((), (), s32[]{:S(2)}) async-start(), calls=%async_computation.2 | async-start | bytes 6684672 | tf_op jit(solution)/shard_map/all_gather | solution.py:294
  12.6 261.2 %all-gather.11.cloned.1.call-start = ((), (), s32[]{:S(2)}) async-start(), calls=%async_computation.4 | async-start | bytes 1114112 | tf_op jit(solution)/shard_map/all_gather | solution.py:310
  13.2 324.0 %reduce-scatter.2.cloned.1.call-start = ((), (), s32[]{:S(2)}) async-start(), calls=%async_computation.5 | async-start | bytes 2228224 | tf_op jit(solution)/shard_map/reduce_scatter | solution.py:311
  273.7 3.4 copy-start.1
Sparse Core Ops, SparseCore 0:
  9.1 67.4 all-gather.8
  78.5 52.7 all-gather.4
  133.7 68.3 all-gather.6
  204.3 47.3 all-gather.10
  277.3 59.8 reduce-scatter.1
